TPU v7x, 32 devices: a whole 2x2x4 slice. The times are simulated.
32 devices in a mesh: dp: 16 (over z, y, core), tensor: 2 (over x).
Axes of the slice: x: 2, y: 2, z: 4, core: 2. Of those that a mesh axis runs over, the one named last changes fastest.
Arguments:
- residual_in: float32 [8192, 1024], P(('dp', 'tensor')), may hold values from -6 to 6
- out_cotangent: float32 [8192, 1024], P(('dp', 'tensor')), may hold values from -6 to 6
- seq_lengths: int32 [4], replicated, may hold values from 1 to 4096, 8192 in all
- qkv_weight: float32 [1024, 3072], P('dp', 'tensor'), may hold values from -1 to 1
- out_weight: float32 [1024, 1024], P('tensor', 'dp'), may hold values from -2 to 2
- in_weight: float32 [1024, 2, 2624], P('dp', None, 'tensor'), may hold values from -0.1875 to 0.1875
- down_weight: float32 [2624, 1024], P('tensor', 'dp'), may hold values from -0.125 to 0.125
- norm_gains: float32 [2, 1024], replicated, may hold values from 0.5 to 1.5
- qkv_moments: float32 [2, 1024, 3072], P(None, 'dp', 'tensor'), may hold values from -8192 to 8192, as said below
- out_moments: float32 [2, 1024, 1024], P(None, 'tensor', 'dp'), may hold values from -8192 to 8192, as said below
- in_moments: float32 [2, 1024, 2, 2624], P(None, 'dp', None, 'tensor'), may hold values from -8192 to 8192, as said below
- down_moments: float32 [2, 2624, 1024], P(None, 'tensor', 'dp'), may hold values from -8192 to 8192, as said below
- gain_moments: float32 [2, 2, 1024], replicated, may hold values from -8192 to 8192, as said below
Outputs:
- block_out: float32 [8192, 1024], P(('dp', 'tensor'))
- residual_grad: float32 [8192, 1024], P(('dp', 'tensor'))
- qkv_grad: float32 [1024, 3072], P('dp', 'tensor')
- out_weight_grad: float32 [1024, 1024], P('tensor', 'dp')
- in_grad: float32 [1024, 2, 2624], P('dp', None, 'tensor')
- down_grad: float32 [2624, 1024], P('tensor', 'dp')
- gains_grad: float32 [2, 1024], replicated
- new_qkv: float32 [1024, 3072], P('dp', 'tensor')
- new_out: float32 [1024, 1024], P('tensor', 'dp')
- new_in: float32 [1024, 2, 2624], P('dp', None, 'tensor')
- new_down: float32 [2624, 1024], P('tensor', 'dp')
- new_gains: float32 [2, 1024], replicated
- new_qkv_moments: float32 [2, 1024, 3072], P(None, 'dp', 'tensor')
- new_out_moments: float32 [2, 1024, 1024], P(None, 'tensor', 'dp')
- new_in_moments: float32 [2, 1024, 2, 2624], P(None, 'dp', None, 'tensor')
- new_down_moments: float32 [2, 2624, 1024], P(None, 'tensor', 'dp')
- new_gain_moments: float32 [2, 2, 1024], replicated
Inputs may be any that keep to these rules, and one draw needn't show every extreme that they name: `seq_lengths`: the lengths sum to 8192; the longest is exactly 4096. `qkv_moments`: index 0 is the first moment, index 1 the second moment, which is positive. `out_moments`: index 0 is the first moment, index 1 the second moment, which is positive. `in_moments`: index 0 is the first moment, index 1 the second moment, which is positive. `down_moments`: index 0 is the first moment, index 1 the second moment, which is positive. `gain_moments`: index 0 is the first moment, index 1 the second moment, which is positive.
All inputs are finite; a program needn't handle non-finite values.
Results may differ from a plain program's by a relative error of at most 0.019.
Values may be sent and summed in bfloat16 or wider, within the bound.
A program may use at most 128 MiB of HBM per device.

v0:
```python
import math
import jax
import jax.numpy as jnp
from jax import lax
from jax.sharding import PartitionSpec as P

HD = 64
HALF_WIN = 64
STEP = 3
NORM_EPS = 1e-05
ROPE_BASE = 10000.0
BETA_ONE = 0.9
BETA_TWO = 0.999
ADAM_EPS = 1e-08
LEARN_RATE = 0.005
DECAY_RATE = 0.1
MASKED = -1e30


def padded(value, sides, width):
    for axis, dim in sides:
        size, length = (lax.axis_size(axis), value.shape[dim])
        up = [(i, (i + 1) % size) for i in range(size - 1)]
        down = [(j, i) for i, j in up]
        last = lax.slice_in_dim(value, length - width, length, axis=dim)
        first = lax.slice_in_dim(value, 0, width, axis=dim)
        before = lax.ppermute(last, axis, up)
        after = lax.ppermute(first, axis, down)
        value = jnp.concatenate([before, value, after], axis=dim)
    return value


def norm_forward(rows, gain):
    row_mean = jnp.mean(rows, axis=-1, keepdims=True)
    centered = rows - row_mean
    inv_std = lax.rsqrt(jnp.mean(centered * centered, axis=-1, keepdims=True) + NORM_EPS)
    normed = centered * inv_std
    return (normed, inv_std, normed * gain)


def norm_backward(grad_out, normed, inv_std, gain):
    scaled = grad_out * gain
    grad_rows = inv_std * (
        scaled
        - jnp.mean(scaled, axis=-1, keepdims=True)
        - normed * jnp.mean(scaled * normed, axis=-1, keepdims=True)
    )
    return (grad_rows, jnp.sum(grad_out * normed, axis=0))


def seq_coords(seq_lengths, places):
    seq_ends = jnp.cumsum(seq_lengths, dtype=jnp.int32)
    passed = (seq_ends[None, :] <= places[:, None]).astype(jnp.int32)
    seq_ids = jnp.sum(passed, axis=1, dtype=jnp.int32)
    seq_start = jnp.sum(passed * seq_lengths[None, :], axis=1, dtype=jnp.int32)
    return (seq_ids, places - seq_start)


def rotary_tables(offsets, head_dim):
    half_dim = head_dim // 2
    inv_freq = ROPE_BASE ** (-2.0 * jnp.arange(half_dim).astype(jnp.float32) / head_dim)
    angles = offsets.astype(jnp.float32)[:, None] * inv_freq[None, :]
    cos_table = jnp.cos(angles)
    sin_table = jnp.sin(angles)
    return (
        jnp.concatenate([cos_table, cos_table], axis=-1),
        jnp.concatenate([sin_table, sin_table], axis=-1),
    )


def rotate(feats, cos_table, sin_table):
    half_dim = feats.shape[-1] // 2
    turned = jnp.concatenate([-feats[..., half_dim:], feats[..., :half_dim]], axis=-1)
    return feats * cos_table[:, None, :] + turned * sin_table[:, None, :]


def unrotate(grads, cos_table, sin_table):
    half_dim = grads.shape[-1] // 2
    spun = grads * sin_table[:, None, :]
    back = jnp.concatenate([spun[..., half_dim:], -spun[..., :half_dim]], axis=-1)
    return grads * cos_table[:, None, :] + back


def gelu_parts(pre_act):
    normal_cdf = 0.5 * (1.0 + lax.erf(pre_act * (1.0 / math.sqrt(2.0))))
    density = jnp.exp(-0.5 * pre_act * pre_act) * (1.0 / math.sqrt(2.0 * math.pi))
    return (pre_act * normal_cdf, normal_cdf + pre_act * density)


def block_mask(query_ids, key_ids, reach):
    query_count = query_ids.shape[0]
    key_count = key_ids.shape[0]
    distance = (
        jnp.arange(key_count, dtype=jnp.int32)[None, :]
        - reach
        - jnp.arange(query_count, dtype=jnp.int32)[:, None]
    )
    return (query_ids[:, None] == key_ids[None, :]) & (jnp.abs(distance) <= reach)


def block_scores(query_rows, key_rows, allowed):
    score_scale = 1.0 / math.sqrt(query_rows.shape[-1])
    scores = (
        jnp.einsum("qhe,khe->hqk", query_rows, key_rows, preferred_element_type=jnp.float32)
        * score_scale
    )
    return jnp.where(allowed[None, :, :], scores, MASKED)


def block_forward(query_rows, key_rows, value_rows, allowed):
    scores = block_scores(query_rows, key_rows, allowed)
    row_max = jnp.max(scores, axis=-1, keepdims=True)
    log_norm = row_max + jnp.log(jnp.sum(jnp.exp(scores - row_max), axis=-1, keepdims=True))
    attn_probs = jnp.exp(scores - log_norm).astype(jnp.bfloat16)
    mixed = jnp.einsum("hqk,khe->qhe", attn_probs, value_rows, preferred_element_type=jnp.float32)
    return (mixed.astype(jnp.bfloat16), log_norm[..., 0])


def block_backward(query_rows, key_rows, value_rows, allowed, log_norm, grad_rows, deltas):
    score_scale = 1.0 / math.sqrt(query_rows.shape[-1])
    scores = block_scores(query_rows, key_rows, allowed)
    probs_full = jnp.exp(scores - log_norm[..., None])
    grad_probs = jnp.einsum(
        "qhe,khe->hqk", grad_rows, value_rows, preferred_element_type=jnp.float32
    )
    grad_scores = (probs_full * (grad_probs - jnp.transpose(deltas)[:, :, None])).astype(
        jnp.bfloat16
    )
    attn_probs = probs_full.astype(jnp.bfloat16)
    grad_queries = (
        jnp.einsum("hqk,khe->qhe", grad_scores, key_rows, preferred_element_type=jnp.float32)
        * score_scale
    )
    grad_keys = (
        jnp.einsum("hqk,qhe->khe", grad_scores, query_rows, preferred_element_type=jnp.float32)
        * score_scale
    )
    grad_values = jnp.einsum(
        "hqk,qhe->khe", attn_probs, grad_rows, preferred_element_type=jnp.float32
    )
    return (grad_queries, grad_keys, grad_values)


def product_rows(matrix, weight, contract_dim):
    return lax.dot_general(
        matrix, weight, (((1,), (contract_dim,)), ((), ())), preferred_element_type=jnp.float32
    )


def across_rows(left, right):
    return lax.dot_general(
        left, right, (((0,), (0,)), ((), ())), preferred_element_type=jnp.float32
    )


def against_cols(left, right):
    return lax.dot_general(
        left, right, (((1,), (1,)), ((), ())), preferred_element_type=jnp.float32
    )


def adam_update(weight, moments, grad, decay):
    first_moment = BETA_ONE * moments[0] + (1.0 - BETA_ONE) * grad
    second_moment = BETA_TWO * moments[1] + (1.0 - BETA_TWO) * grad * grad
    first_hat = first_moment / (1.0 - BETA_ONE**STEP)
    second_hat = second_moment / (1.0 - BETA_TWO**STEP)
    new_weight = weight - LEARN_RATE * (
        first_hat / (jnp.sqrt(second_hat) + ADAM_EPS) + decay * weight
    )
    return (new_weight, jnp.stack([first_moment, second_moment]))


def local(
    residual_in,
    out_cotangent,
    seq_lengths,
    qkv_weight,
    out_weight,
    in_weight,
    down_weight,
    norm_gains,
    qkv_moments,
    out_moments,
    in_moments,
    down_moments,
    gain_moments,
):
    tensor_count = lax.axis_size("tensor")
    data_count = lax.axis_size("dp")
    local_rows = residual_in.shape[0]
    seq_rows = local_rows * tensor_count
    reach = HALF_WIN
    block_rows = min(512, seq_rows)
    span = block_rows + 2 * reach
    qkv_full, out_full, in_full, down_full = (
        lax.all_gather(qkv_weight.astype(jnp.bfloat16), "dp", axis=0, tiled=True),
        lax.all_gather(out_weight.astype(jnp.bfloat16), "dp", axis=1, tiled=True),
        lax.all_gather(in_weight.astype(jnp.bfloat16), "dp", axis=0, tiled=True),
        lax.all_gather(down_weight.astype(jnp.bfloat16), "dp", axis=1, tiled=True),
    )
    model_dim = qkv_full.shape[0]
    head_dim = HD
    local_heads = qkv_full.shape[1] // (3 * head_dim)
    local_hidden = in_full.shape[2]
    head_feats = local_heads * head_dim
    in_flat = in_full.reshape(model_dim, 2 * local_hidden)
    first_token = lax.axis_index("dp") * seq_rows
    places = first_token + jnp.arange(seq_rows, dtype=jnp.int32)
    query_ids, offsets = seq_coords(seq_lengths, places)
    cos_table, sin_table = rotary_tables(offsets, head_dim)
    key_places = first_token - reach + jnp.arange(seq_rows + 2 * reach, dtype=jnp.int32)
    inside = (key_places >= 0) & (key_places < seq_rows * data_count)
    key_ids = jnp.where(inside, seq_coords(seq_lengths, key_places)[0], -1)
    first_normed, first_inv, first_scaled = norm_forward(residual_in, norm_gains[0])
    normed_in = lax.all_gather(first_scaled.astype(jnp.bfloat16), "tensor", axis=0, tiled=True)
    proj = jnp.dot(normed_in, qkv_full, preferred_element_type=jnp.float32).reshape(
        seq_rows, local_heads, 3, head_dim
    )
    queries = rotate(proj[:, :, 0], cos_table, sin_table).astype(jnp.bfloat16)
    keys = rotate(proj[:, :, 1], cos_table, sin_table).astype(jnp.bfloat16)
    values = proj[:, :, 2].astype(jnp.bfloat16)
    key_vals = jnp.concatenate(
        [keys.reshape(seq_rows, head_feats), values.reshape(seq_rows, head_feats)], axis=1
    )
    key_vals_pad = padded(key_vals, (("dp", 0),), reach)
    keys_pad = key_vals_pad[:, :head_feats].reshape(seq_rows + 2 * reach, local_heads, head_dim)
    values_pad = key_vals_pad[:, head_feats:].reshape(seq_rows + 2 * reach, local_heads, head_dim)
    allowed = block_mask(query_ids, key_ids, reach)
    mixed_part, norm_part = block_forward(queries, keys_pad, values_pad, allowed)
    mixed_flat = mixed_part.reshape(seq_rows, head_feats)
    attn_out = lax.psum_scatter(
        product_rows(mixed_flat, out_full, 0), "tensor", scatter_dimension=0, tiled=True
    )
    middle = residual_in + attn_out
    second_normed, second_inv, second_scaled = norm_forward(middle, norm_gains[1])
    ffn_in = lax.all_gather(second_scaled.astype(jnp.bfloat16), "tensor", axis=0, tiled=True)
    both = jnp.dot(ffn_in, in_flat, preferred_element_type=jnp.float32).reshape(
        seq_rows, 2, local_hidden
    )
    activated, slope = gelu_parts(both[:, 0])
    gated = (activated * both[:, 1]).astype(jnp.bfloat16)
    ffn_out = lax.psum_scatter(
        product_rows(gated, down_full, 0).astype(jnp.bfloat16),
        "tensor",
        scatter_dimension=0,
        tiled=True,
    ).astype(jnp.float32)
    block_out = middle + ffn_out
    grad_out_all = lax.all_gather(out_cotangent.astype(jnp.bfloat16), "tensor", axis=0, tiled=True)
    grad_gated = against_cols(grad_out_all, down_full)
    down_grad_part = across_rows(gated, grad_out_all)
    grad_both = jnp.stack([grad_gated * both[:, 1] * slope, grad_gated * activated], axis=1)
    grad_both_flat = grad_both.astype(jnp.bfloat16).reshape(seq_rows, 2 * local_hidden)
    in_grad_part = across_rows(ffn_in, grad_both_flat).reshape(model_dim, 2, local_hidden)
    grad_ffn_in = lax.psum_scatter(
        product_rows(grad_both_flat, in_flat, 1), "tensor", scatter_dimension=0, tiled=True
    )
    grad_second, second_gain_part = norm_backward(
        grad_ffn_in, second_normed, second_inv, norm_gains[1]
    )
    grad_middle = out_cotangent + grad_second
    middle_all = lax.all_gather(grad_middle.astype(jnp.bfloat16), "tensor", axis=0, tiled=True)
    out_grad_part = across_rows(mixed_flat, middle_all)
    grad_mixed = (
        against_cols(middle_all, out_full)
        .astype(jnp.bfloat16)
        .reshape(seq_rows, local_heads, head_dim)
    )
    deltas = jnp.sum(grad_mixed.astype(jnp.float32) * mixed_part.astype(jnp.float32), axis=-1)
    grad_kv_pad = jnp.zeros((seq_rows + 2 * reach, 2 * head_feats), jnp.float32)
    allowed = block_mask(query_ids, key_ids, reach)
    grad_q, grad_k, grad_v = block_backward(
        queries, keys_pad, values_pad, allowed, norm_part, grad_mixed, deltas
    )
    update = jnp.concatenate(
        [grad_k.reshape(span, head_feats), grad_v.reshape(span, head_feats)], axis=1
    )
    grad_kv_pad = grad_kv_pad.at[0:span].add(update)
    edge_grads = jnp.concatenate([grad_kv_pad[:reach], grad_kv_pad[seq_rows + reach :]], axis=0)
    edge_ext = padded(edge_grads.astype(jnp.bfloat16), (("dp", 0),), reach).astype(edge_grads.dtype)
    own_grads = grad_kv_pad[reach : reach + seq_rows]
    own_grads = own_grads.at[:reach].add(edge_ext[:reach])
    own_grads = own_grads.at[seq_rows - reach :].add(edge_ext[3 * reach :])
    grad_keys = own_grads[:, :head_feats].reshape(seq_rows, local_heads, head_dim)
    grad_values = own_grads[:, head_feats:].reshape(seq_rows, local_heads, head_dim)
    grad_proj = jnp.stack(
        [
            unrotate(grad_q, cos_table, sin_table),
            unrotate(grad_keys, cos_table, sin_table),
            grad_values,
        ],
        axis=2,
    )
    grad_proj_flat = grad_proj.astype(jnp.bfloat16).reshape(seq_rows, 3 * head_feats)
    qkv_grad_part = across_rows(normed_in, grad_proj_flat)
    grad_norm_in = lax.psum_scatter(
        product_rows(grad_proj_flat, qkv_full, 1).astype(jnp.bfloat16),
        "tensor",
        scatter_dimension=0,
        tiled=True,
    ).astype(jnp.float32)
    grad_first, first_gain_part = norm_backward(
        grad_norm_in, first_normed, first_inv, norm_gains[0]
    )
    residual_grad = grad_middle + grad_first
    gains_grad = lax.psum(jnp.stack([first_gain_part, second_gain_part]), ("dp", "tensor"))
    qkv_grad, out_weight_grad, in_grad, down_grad = (
        lax.psum_scatter(
            qkv_grad_part.astype(jnp.bfloat16), "dp", scatter_dimension=0, tiled=True
        ).astype(jnp.float32),
        lax.psum_scatter(
            out_grad_part.astype(jnp.bfloat16), "dp", scatter_dimension=1, tiled=True
        ).astype(jnp.float32),
        lax.psum_scatter(
            in_grad_part.astype(jnp.bfloat16), "dp", scatter_dimension=0, tiled=True
        ).astype(jnp.float32),
        lax.psum_scatter(
            down_grad_part.astype(jnp.bfloat16), "dp", scatter_dimension=1, tiled=True
        ).astype(jnp.float32),
    )
    new_qkv, new_qkv_moments = adam_update(qkv_weight, qkv_moments, qkv_grad, DECAY_RATE)
    new_out, new_out_moments = adam_update(out_weight, out_moments, out_weight_grad, DECAY_RATE)
    new_in, new_in_moments = adam_update(in_weight, in_moments, in_grad, DECAY_RATE)
    new_down, new_down_moments = adam_update(down_weight, down_moments, down_grad, DECAY_RATE)
    new_gains, new_gain_moments = adam_update(norm_gains, gain_moments, gains_grad, 0.0)
    return (
        block_out,
        residual_grad,
        qkv_grad,
        out_weight_grad,
        in_grad,
        down_grad,
        gains_grad,
        new_qkv,
        new_out,
        new_in,
        new_down,
        new_gains,
        new_qkv_moments,
        new_out_moments,
        new_in_moments,
        new_down_moments,
        new_gain_moments,
    )


def solution(mesh):
    return jax.shard_map(
        local,
        mesh=mesh,
        in_specs=(
            P(("dp", "tensor"), None),
            P(("dp", "tensor"), None),
            P(),
            P("dp", "tensor"),
            P("tensor", "dp"),
            P("dp", None, "tensor"),
            P("tensor", "dp"),
            P(),
            P(None, "dp", "tensor"),
            P(None, "tensor", "dp"),
            P(None, "dp", None, "tensor"),
            P(None, "tensor", "dp"),
            P(),
        ),
        out_specs=(
            P(("dp", "tensor"), None),
            P(("dp", "tensor"), None),
            P("dp", "tensor"),
            P("tensor", "dp"),
            P("dp", None, "tensor"),
            P("tensor", "dp"),
            P(),
            P("dp", "tensor"),
            P("tensor", "dp"),
            P("dp", None, "tensor"),
            P("tensor", "dp"),
            P(),
            P(None, "dp", "tensor"),
            P(None, "tensor", "dp"),
            P(None, "dp", None, "tensor"),
            P(None, "tensor", "dp"),
            P(),
        ),
        check_vma=False,
    )
```

profile of v0, /device:TPU:0, one launch (start us, length us, event | category | flops | bytes accessed | tf_op | source)
XLA Modules:
  0.0 752.0 jit_solution(12880494471490557528)
XLA Ops:
  15.8 20.5 %all-gather.9.cloned.1.call-done = bf16[512,1024]{1,0:T(8,128)(2,1)} async-done(((bf16[256,1024]{1,0:T(8,128)(2,1)}), bf16[512,1024]{1,0:T(8,128)(2,1)}) %all-gather.9.cloned.1.call-update) | async-done | bytes 1048592 | tf_op jit(solution)/shard_map/all_gather | solution.py:215
  36.2 48.3 %all-gather.11.cloned.1.call-done = bf16[1024,1536]{1,0:T(8,128)(2,1)} async-done(((bf16[64,1536]{1,0:T(8,128)(2,1)}), bf16[1024,1536]{1,0:T(8,128)(2,1)}) %all-gather.11.cloned.1.call-update) | async-done | bytes 3145744 | tf_op jit(solution)/shard_map/all_gather | solution.py:196
  106.3 18.5 %all-gather.13.cloned.1.call-done = bf16[512,1024]{0,1:T(8,128)(2,1)} async-done(((bf16[512,64]{0,1:T(8,128)(2,1)}), bf16[512,1024]{0,1:T(8,128)(2,1)}) %all-gather.13.cloned.1.call-update) | async-done | bytes 1048592 | tf_op jit(solution)/shard_map/all_gather | solution.py:197
  129.3 29.9 %reduce-scatter.9.cloned.1.call-done = f32[256,1024]{1,0:T(8,128)} async-done(((f32[512,1024]{1,0:T(8,128)}), f32[256,1024]{1,0:T(8,128)}) %reduce-scatter.9.cloned.1.call-update) | async-done | bytes 1048592 | tf_op jit(solution)/shard_map/reduce_scatter | solution.py:231
  163.0 57.7 %all-gather.17.cloned.1.call-done = bf16[1024,2,1312]{2,0,1:T(8,128)(2,1)} async-done(((bf16[64,2,1312]{2,0,1:T(8,128)(2,1)}), bf16[1024,2,1312]{2,0,1:T(8,128)(2,1)}) %all-gather.17.cloned.1.call-update) | async-done | bytes 5373968 | tf_op jit(solution)/shard_map/all_gather | solution.py:198
  220.7 8.1 %copy.60 = bf16[1024,2,1312]{0,2,1:T(8,128)(2,1)} copy(bf16[1024,2,1312]{2,0,1:T(8,128)(2,1)} %all-gather.17.cloned.1.call-done) | data formatting | bytes 10747904 | tf_op jit(solution)/shard_map/all_gather | solution.py:198
  228.8 13.8 %all-gather.15.cloned.1.call-done = bf16[512,1024]{1,0:T(8,128)(2,1)} async-done(((bf16[256,1024]{1,0:T(8,128)(2,1)}), bf16[512,1024]{1,0:T(8,128)(2,1)}) %all-gather.15.cloned.1.call-update) | async-done | bytes 1048592 | tf_op jit(solution)/shard_map/all_gather | solution.py:236
  242.6 5.3 fusion.2
  252.0 14.1 %all-gather.21.cloned.1.call-done = bf16[512,1024]{1,0:T(8,128)(2,1)} async-done(((bf16[256,1024]{1,0:T(8,128)(2,1)}), bf16[512,1024]{1,0:T(8,128)(2,1)}) %all-gather.21.cloned.1.call-update) | async-done | bytes 1048592 | tf_op jit(solution)/shard_map/all_gather | solution.py:249
  271.2 65.3 %reduce-scatter.23.cloned.1.call-done = bf16[1312,64]{0,1:T(8,128)(2,1)} async-done(((bf16[1312,1024]{0,1:T(8,128)(2,1)}), bf16[1312,64]{0,1:T(8,128)(2,1)}) %reduce-scatter.23.cloned.1.call-update) | async-done | bytes 167952 | tf_op jit(solution)/shard_map/reduce_scatter | solution.py:317
  341.7 43.1 %all-gather.19.cloned.1.call-done = bf16[1312,1024]{0,1:T(8,128)(2,1)} async-done(((bf16[1312,64]{0,1:T(8,128)(2,1)}), bf16[1312,1024]{0,1:T(8,128)(2,1)}) %all-gather.19.cloned.1.call-update) | async-done | bytes 2686992 | tf_op jit(solution)/shard_map/all_gather | solution.py:199
  384.8 6.5 fusion.9
  392.7 7.2 convolution_bitcast_fusion
  405.3 25.3 %reduce-scatter.13.cloned.1.call-done = f32[256,1024]{1,0:T(8,128)} async-done(((f32[512,1024]{1,0:T(8,128)}), f32[256,1024]{1,0:T(8,128)}) %reduce-scatter.13.cloned.1.call-update) | async-done | bytes 1048592 | tf_op jit(solution)/shard_map/reduce_scatter | solution.py:255
  432.9 20.9 %reduce-scatter.11.cloned.1.call-done = bf16[256,1024]{1,0:T(8,128)(2,1)} async-done(((bf16[512,1024]{1,0:T(8,128)(2,1)}), bf16[256,1024]{1,0:T(8,128)(2,1)}) %reduce-scatter.11.cloned.1.call-update) | async-done | bytes 524304 | tf_op jit(solution)/shard_map/reduce_scatter | solution.py:242
  457.3 21.4 %all-gather.23.cloned.1.call-done = bf16[512,1024]{1,0:T(8,128)(2,1)} async-done(((bf16[256,1024]{1,0:T(8,128)(2,1)}), bf16[512,1024]{1,0:T(8,128)(2,1)}) %all-gather.23.cloned.1.call-update) | async-done | bytes 1048592 | tf_op jit(solution)/shard_map/all_gather | solution.py:262
  481.1 5.6 fusion.57
  486.8 6.7 multiply_convert_fusion
  529.8 6.4 convolution_convert_fusion
  545.8 19.0 %reduce-scatter.19.cloned.1.call-done = bf16[512,64]{0,1:T(8,128)(2,1)} async-done(((bf16[512,1024]{0,1:T(8,128)(2,1)}), bf16[512,64]{0,1:T(8,128)(2,1)}) %reduce-scatter.19.cloned.1.call-update) | async-done | bytes 65552 | tf_op jit(solution)/shard_map/reduce_scatter | solution.py:311
  568.3 18.6 %reduce-scatter.15.cloned.1.call-done = bf16[256,1024]{1,0:T(8,128)(2,1)} async-done(((bf16[512,1024]{1,0:T(8,128)(2,1)}), bf16[256,1024]{1,0:T(8,128)(2,1)}) %reduce-scatter.15.cloned.1.call-update) | async-done | bytes 524304 | tf_op jit(solution)/shard_map/reduce_scatter | solution.py:296
  590.3 40.4 %psum.7 = f32[2,1024]{1,0:T(2,128)} all-reduce(f32[2,1024]{1,0:T(2,128)} %pad_maximum_fusion.12), channel_id=1, replica_groups=mesh['dp'=16,'tensor'=2] {'dp','tensor'}, use_global_device_ids=true, to_apply=%region_25.26 | all-reduce | flops 2048 | bytes 16384 | tf_op jit(solution)/shard_map/psum | solution.py:306
  636.4 36.2 %reduce-scatter.21.cloned.1.call-done = bf16[64,2,1312]{2,0,1:T(8,128)(2,1)} async-done(((bf16[1024,2,1312]{2,0,1:T(8,128)(2,1)}), bf16[64,2,1312]{2,0,1:T(8,128)(2,1)}) %reduce-scatter.21.cloned.1.call-update) | async-done | bytes 335888 | tf_op jit(solution)/shard_map/reduce_scatter | solution.py:314
  679.5 62.4 %reduce-scatter.17.cloned.1.call-done = bf16[64,1536]{1,0:T(8,128)(2,1)} async-done(((bf16[1024,1536]{1,0:T(8,128)(2,1)}), bf16[64,1536]{1,0:T(8,128)(2,1)}) %reduce-scatter.17.cloned.1.call-update) | async-done | bytes 196624 | tf_op jit(solution)/shard_map/reduce_scatter | solution.py:308
  (225 shorter events, 135.3 us)
Async XLA Ops:
  7.2 29.0 %all-gather.9.cloned.1.call-start = ((), (), s32[]{:S(2)}) async-start(), calls=%async_computation.8 | async-start | bytes 1572864 | tf_op jit(solution)/shard_map/all_gather | solution.py:215
  10.2 78.4 %copy-start.37 = (f32[256]{0:T(256)}, f32[256]{0:T(256)S(1)}, u32[]{:S(2)}) copy-start(f32[256]{0:T(256)S(1)} %add_rsqrt_fusion.1) | copy-start | bytes 3076
  12.1 72.5 %all-gather.11.cloned.1.call-start = ((), (), s32[]{:S(2)}) async-start(), calls=%async_computation.9 | async-start | bytes 3342336 | tf_op jit(solution)/shard_map/all_gather | solution.py:196
  12.9 112.0 %all-gather.13.cloned.1.call-start = ((), (), s32[]{:S(2)}) async-start(), calls=%async_computation.10 | async-start | bytes 1114112 | tf_op jit(solution)/shard_map/all_gather | solution.py:197
  13.6 145.7 %reduce-scatter.9.cloned.1.call-start = ((), (), s32[]{:S(2)}) async-start(), calls=%async_computation.11 | async-start | bytes 3145728 | tf_op jit(solution)/shard_map/reduce_scatter | solution.py:231
  90.3 3.9 collective-permute-start
  92.4 3.4 collective-permute-start.1
  128.2 92.5 %all-gather.17.cloned.1.call-start = ((), (), s32[]{:S(2)}) async-start(), calls=%async_computation.13 | async-start | bytes 6127616 | tf_op jit(solution)/shard_map/all_gather | solution.py:198
  129.3 113.3 %all-gather.15.cloned.1.call-start = ((), (), s32[]{:S(2)}) async-start(), calls=%async_computation.12 | async-start | bytes 1572864 | tf_op jit(solution)/shard_map/all_gather | solution.py:236
  162.0 104.1 %all-gather.21.cloned.1.call-start = ((), (), s32[]{:S(2)}) async-start(), calls=%async_computation.16 | async-start | bytes 1572864 | tf_op jit(solution)/shard_map/all_gather | solution.py:249
  162.9 173.6 %reduce-scatter.23.cloned.1.call-start = ((), (), s32[]{:S(2)}) async-start(), calls=%async_computation.23 | async-start | bytes 3063808 | tf_op jit(solution)/shard_map/reduce_scatter | solution.py:317
  271.2 113.6 %all-gather.19.cloned.1.call-start = ((), (), s32[]{:S(2)}) async-start(), calls=%async_computation.14 | async-start | bytes 3063808 | tf_op jit(solution)/shard_map/all_gather | solution.py:199
  341.6 89.0 %reduce-scatter.13.cloned.1.call-start = ((), (), s32[]{:S(2)}) async-start(), calls=%async_computation.17 | async-start | bytes 3145728 | tf_op jit(solution)/shard_map/reduce_scatter | solution.py:255
  400.0 53.9 %reduce-scatter.11.cloned.1.call-start = ((), (), s32[]{:S(2)}) async-start(), calls=%async_computation.15 | async-start | bytes 1572864 | tf_op jit(solution)/shard_map/reduce_scatter | solution.py:242
  405.3 73.4 %all-gather.23.cloned.1.call-start = ((), (), s32[]{:S(2)}) async-start(), calls=%async_computation.18 | async-start | bytes 1572864 | tf_op jit(solution)/shard_map/all_gather | solution.py:262
  457.2 107.5 %reduce-scatter.19.cloned.1.call-start = ((), (), s32[]{:S(2)}) async-start(), calls=%async_computation.21 | async-start | bytes 1114112 | tf_op jit(solution)/shard_map/reduce_scatter | solution.py:311
  499.5 10.1 %collective-permute-start.2 = (bf16[64,1024]{0,1:T(8,128)(2,1)}, bf16[64,1024]{0,1:T(8,128)(2,1)}, u32[]{:S(2)}, u32[]{:S(2)}) collective-permute-start(bf16[64,1024]{0,1:T(8,128)(2,1)} %get-tuple-element.137), channel_id=1, source_target_pairs={{0,2},{2,4},{4,6},{6,8},{8,10},{10,12},{12,14},{14,16},{16,18},{18... | collective-permute-start | bytes 393224 | tf_op jit(solution)/shard_map/ppermute | solution.py:27
  501.8 7.8 %collective-permute-start.3 = (bf16[64,1024]{0,1:T(8,128)(2,1)}, bf16[64,1024]{0,1:T(8,128)(2,1)}, u32[]{:S(2)}, u32[]{:S(2)}) collective-permute-start(bf16[64,1024]{0,1:T(8,128)(2,1)} %get-tuple-element.138), channel_id=1, source_target_pairs={{2,0},{4,2},{6,4},{8,6},{10,8},{12,10},{14,12},{16,14},{18,16},{20... | collective-permute-start | bytes 393224 | tf_op jit(solution)/shard_map/ppermute | solution.py:28
  505.0 81.9 %reduce-scatter.15.cloned.1.call-start = ((), (), s32[]{:S(2)}) async-start(), calls=%async_computation.19 | async-start | bytes 1572864 | tf_op jit(solution)/shard_map/reduce_scatter | solution.py:296
  529.7 142.9 %reduce-scatter.21.cloned.1.call-start = ((), (), s32[]{:S(2)}) async-start(), calls=%async_computation.22 | async-start | bytes 6127616 | tf_op jit(solution)/shard_map/reduce_scatter | solution.py:314
  536.2 205.7 %reduce-scatter.17.cloned.1.call-start = ((), (), s32[]{:S(2)}) async-start(), calls=%async_computation.20 | async-start | bytes 3342336 | tf_op jit(solution)/shard_map/reduce_scatter | solution.py:308
  544.9 85.8 %copy-start.36 = (f32[2,1024]{1,0:T(2,128)S(1)}, f32[2,1024]{1,0:T(2,128)}, u32[]{:S(2)}) copy-start(f32[2,1024]{1,0:T(2,128)} %param.28) | copy-start | bytes 24580
  544.9 89.2 %copy-start.9 = (f32[256,1024]{1,0:T(8,128)S(1)}, f32[256,1024]{1,0:T(8,128)}, u32[]{:S(2)}) copy-start(f32[256,1024]{1,0:T(8,128)} %get-tuple-element.127) | copy-start | bytes 3145732
  568.3 104.4 %copy-start.13 = (f32[64,2,1312]{2,1,0:T(2,128)S(1)}, f32[64,2,1312]{2,1,0:T(2,128)}, u32[]{:S(2)}) copy-start(f32[64,2,1312]{2,1,0:T(2,128)} %param.26) | copy-start | bytes 2015236
  (42 other events, 472.3 us)
Sparse Core Ops, SparseCore 0:
  12.2 23.9 all-gather.8
  39.1 45.4 all-gather.10
  87.3 37.4 all-gather.12
  128.4 30.8 reduce-scatter.8
  162.0 58.6 all-gather.16
  222.7 19.9 all-gather.14
  244.7 21.2 all-gather.20
  271.3 65.1 reduce-scatter.22
  341.7 42.9 all-gather.18
  400.1 30.5 reduce-scatter.12
  433.5 20.3 reduce-scatter.10
  457.3 21.2 all-gather.22
  505.1 59.6 reduce-scatter.18
  567.4 19.3 reduce-scatter.14
  590.6 82.0 reduce-scatter.20
  676.3 65.5 reduce-scatter.16
where the time goes:
time: 762 us; the launch traced here: 752 us
  waiting for transfers between devices  517 us (68%)
  matrix products  76.6 us (10%)
  other arithmetic  56 us (7%)
  blocking collectives  40.4 us (5%)
  local copies, waits for them, and re-layouts  38.4 us (5%)
  between operations  15.2 us (2%)
  starting transfers between devices  8.29 us (1%)
    reduce_scatter x1, waiting for transfers between devices, local(): lax.psum_scatter(down_grad_part.astype(jnp.bfloat16), 'dp', scatter_dimen...  65.3 us
    reduce_scatter x1, waiting for transfers between devices, local(): lax.psum_scatter(qkv_grad_part.astype(jnp.bfloat16), 'dp', scatter_dimens...  62.4 us
    all_gather x1, waiting for transfers between devices, local(): lax.all_gather(in_weight.astype(jnp.bfloat16), 'dp', axis=0, tiled=True)  57.7 us
    all_gather x1, waiting for transfers between devices, local(): lax.all_gather(qkv_weight.astype(jnp.bfloat16), 'dp', axis=0, tiled=True)  48.3 us
    all_gather x1, waiting for transfers between devices, local(): lax.all_gather(down_weight.astype(jnp.bfloat16), 'dp', axis=1, tiled=True)  43.1 us
    psum x1, blocking collectives, local(): lax.psum(jnp.stack([first_gain_part, second_gain_part]), ('dp', 'tensor'))  40.4 us
    reduce_scatter x1, waiting for transfers between devices, local(): lax.psum_scatter(in_grad_part.astype(jnp.bfloat16), 'dp', scatter_dimensi...  36.2 us
    reduce_scatter x1, waiting for transfers between devices, local(): lax.psum_scatter(product_rows(mixed_flat, out_full, 0), 'tensor', scatter...  29.9 us
  transfers between devices with their start and end apart: 20, of which 17 were waited for; matrix products, arithmetic and copies ran while one was open for 14% of the time, Pallas kernels for 0%

commit v1 on v0

--- a/solution.py
+++ b/solution.py
@@ -15,6 +15,11 @@
 LEARN_RATE = 0.005
 DECAY_RATE = 0.1
 MASKED = -1e30
+
+
+def one_after_other(array, leading, second):
+    half = lax.psum(array, leading)
+    return lax.psum(half, second)
 
 
 def padded(value, sides, width):
@@ -303,7 +308,7 @@
         grad_norm_in, first_normed, first_inv, norm_gains[0]
     )
     residual_grad = grad_middle + grad_first
-    gains_grad = lax.psum(jnp.stack([first_gain_part, second_gain_part]), ("dp", "tensor"))
+    gains_grad = one_after_other(jnp.stack([first_gain_part, second_gain_part]), "dp", "tensor")
     qkv_grad, out_weight_grad, in_grad, down_grad = (
         lax.psum_scatter(
             qkv_grad_part.astype(jnp.bfloat16), "dp", scatter_dimension=0, tiled=True

time: 762 us -> 761 us (level)
    psum x1 -> x2, blocking collectives: 40.4 us -> 40.2 us  [the longest x1 34.3 us: one_after_other(): half = lax.psum(array, leading)]
where the time goes in v1:
time: 761 us; the launch traced here: 751 us
  waiting for transfers between devices  517 us (68%)
  matrix products  76.6 us (10%)
  other arithmetic  56 us (7%)
  blocking collectives  40.2 us (5%)
  local copies, waits for them, and re-layouts  38.4 us (5%)
  between operations  15.3 us (2%)
  starting transfers between devices  8.29 us (1%)
    reduce_scatter x1, waiting for transfers between devices, local(): lax.psum_scatter(down_grad_part.astype(jnp.bfloat16), 'dp', scatter_dimen...  65.3 us
    reduce_scatter x1, waiting for transfers between devices, local(): lax.psum_scatter(qkv_grad_part.astype(jnp.bfloat16), 'dp', scatter_dimens...  62.5 us
    all_gather x1, waiting for transfers between devices, local(): lax.all_gather(in_weight.astype(jnp.bfloat16), 'dp', axis=0, tiled=True)  57.7 us
    all_gather x1, waiting for transfers between devices, local(): lax.all_gather(qkv_weight.astype(jnp.bfloat16), 'dp', axis=0, tiled=True)  48.3 us
    all_gather x1, waiting for transfers between devices, local(): lax.all_gather(down_weight.astype(jnp.bfloat16), 'dp', axis=1, tiled=True)  43.1 us
    reduce_scatter x1, waiting for transfers between devices, local(): lax.psum_scatter(in_grad_part.astype(jnp.bfloat16), 'dp', scatter_dimensi...  35.8 us
    psum x1, blocking collectives, one_after_other(): half = lax.psum(array, leading)  34.3 us
    reduce_scatter x1, waiting for transfers between devices, local(): lax.psum_scatter(product_rows(mixed_flat, out_full, 0), 'tensor', scatter...  29.9 us
  transfers between devices with their start and end apart: 20, of which 17 were waited for; matrix products, arithmetic and copies ran while one was open for 14% of the time, Pallas kernels for 0%

profile of v1, /device:TPU:0, one launch (start us, length us, event | category | flops | bytes accessed | tf_op | source)
XLA Modules:
  0.0 751.3 jit_solution(10555810147841030355)
XLA Ops:
  15.8 20.5 %all-gather.9.cloned.1.call-done = bf16[512,1024]{1,0:T(8,128)(2,1)} async-done(((bf16[256,1024]{1,0:T(8,128)(2,1)}), bf16[512,1024]{1,0:T(8,128)(2,1)}) %all-gather.9.cloned.1.call-update) | async-done | bytes 1048592 | tf_op jit(solution)/shard_map/all_gather | solution.py:220
  36.2 48.3 %all-gather.11.cloned.1.call-done = bf16[1024,1536]{1,0:T(8,128)(2,1)} async-done(((bf16[64,1536]{1,0:T(8,128)(2,1)}), bf16[1024,1536]{1,0:T(8,128)(2,1)}) %all-gather.11.cloned.1.call-update) | async-done | bytes 3145744 | tf_op jit(solution)/shard_map/all_gather | solution.py:201
  106.2 18.6 %all-gather.13.cloned.1.call-done = bf16[512,1024]{0,1:T(8,128)(2,1)} async-done(((bf16[512,64]{0,1:T(8,128)(2,1)}), bf16[512,1024]{0,1:T(8,128)(2,1)}) %all-gather.13.cloned.1.call-update) | async-done | bytes 1048592 | tf_op jit(solution)/shard_map/all_gather | solution.py:202
  129.3 29.9 %reduce-scatter.9.cloned.1.call-done = f32[256,1024]{1,0:T(8,128)} async-done(((f32[512,1024]{1,0:T(8,128)}), f32[256,1024]{1,0:T(8,128)}) %reduce-scatter.9.cloned.1.call-update) | async-done | bytes 1048592 | tf_op jit(solution)/shard_map/reduce_scatter | solution.py:236
  163.0 57.7 %all-gather.17.cloned.1.call-done = bf16[1024,2,1312]{2,0,1:T(8,128)(2,1)} async-done(((bf16[64,2,1312]{2,0,1:T(8,128)(2,1)}), bf16[1024,2,1312]{2,0,1:T(8,128)(2,1)}) %all-gather.17.cloned.1.call-update) | async-done | bytes 5373968 | tf_op jit(solution)/shard_map/all_gather | solution.py:203
  220.7 8.1 %copy.60 = bf16[1024,2,1312]{0,2,1:T(8,128)(2,1)} copy(bf16[1024,2,1312]{2,0,1:T(8,128)(2,1)} %all-gather.17.cloned.1.call-done) | data formatting | bytes 10747904 | tf_op jit(solution)/shard_map/all_gather | solution.py:203
  228.8 13.8 %all-gather.15.cloned.1.call-done = bf16[512,1024]{1,0:T(8,128)(2,1)} async-done(((bf16[256,1024]{1,0:T(8,128)(2,1)}), bf16[512,1024]{1,0:T(8,128)(2,1)}) %all-gather.15.cloned.1.call-update) | async-done | bytes 1048592 | tf_op jit(solution)/shard_map/all_gather | solution.py:241
  252.0 14.1 %all-gather.21.cloned.1.call-done = bf16[512,1024]{1,0:T(8,128)(2,1)} async-done(((bf16[256,1024]{1,0:T(8,128)(2,1)}), bf16[512,1024]{1,0:T(8,128)(2,1)}) %all-gather.21.cloned.1.call-update) | async-done | bytes 1048592 | tf_op jit(solution)/shard_map/all_gather | solution.py:254
  271.2 65.3 %reduce-scatter.23.cloned.1.call-done = bf16[1312,64]{0,1:T(8,128)(2,1)} async-done(((bf16[1312,1024]{0,1:T(8,128)(2,1)}), bf16[1312,64]{0,1:T(8,128)(2,1)}) %reduce-scatter.23.cloned.1.call-update) | async-done | bytes 167952 | tf_op jit(solution)/shard_map/reduce_scatter | solution.py:322
  341.7 43.1 %all-gather.19.cloned.1.call-done = bf16[1312,1024]{0,1:T(8,128)(2,1)} async-done(((bf16[1312,64]{0,1:T(8,128)(2,1)}), bf16[1312,1024]{0,1:T(8,128)(2,1)}) %all-gather.19.cloned.1.call-update) | async-done | bytes 2686992 | tf_op jit(solution)/shard_map/all_gather | solution.py:204
  384.7 6.5 fusion.9
  392.7 7.2 convolution_bitcast_fusion
  405.3 25.3 %reduce-scatter.13.cloned.1.call-done = f32[256,1024]{1,0:T(8,128)} async-done(((f32[512,1024]{1,0:T(8,128)}), f32[256,1024]{1,0:T(8,128)}) %reduce-scatter.13.cloned.1.call-update) | async-done | bytes 1048592 | tf_op jit(solution)/shard_map/reduce_scatter | solution.py:260
  432.9 20.9 %reduce-scatter.11.cloned.1.call-done = bf16[256,1024]{1,0:T(8,128)(2,1)} async-done(((bf16[512,1024]{1,0:T(8,128)(2,1)}), bf16[256,1024]{1,0:T(8,128)(2,1)}) %reduce-scatter.11.cloned.1.call-update) | async-done | bytes 524304 | tf_op jit(solution)/shard_map/reduce_scatter | solution.py:247
  457.2 21.4 %all-gather.23.cloned.1.call-done = bf16[512,1024]{1,0:T(8,128)(2,1)} async-done(((bf16[256,1024]{1,0:T(8,128)(2,1)}), bf16[512,1024]{1,0:T(8,128)(2,1)}) %all-gather.23.cloned.1.call-update) | async-done | bytes 1048592 | tf_op jit(solution)/shard_map/all_gather | solution.py:267
  481.1 5.6 fusion.57
  486.8 6.7 multiply_convert_fusion
  529.8 6.4 convolution_convert_fusion
  545.8 18.9 %reduce-scatter.19.cloned.1.call-done = bf16[512,64]{0,1:T(8,128)(2,1)} async-done(((bf16[512,1024]{0,1:T(8,128)(2,1)}), bf16[512,64]{0,1:T(8,128)(2,1)}) %reduce-scatter.19.cloned.1.call-update) | async-done | bytes 65552 | tf_op jit(solution)/shard_map/reduce_scatter | solution.py:316
  568.2 18.6 %reduce-scatter.15.cloned.1.call-done = bf16[256,1024]{1,0:T(8,128)(2,1)} async-done(((bf16[512,1024]{1,0:T(8,128)(2,1)}), bf16[256,1024]{1,0:T(8,128)(2,1)}) %reduce-scatter.15.cloned.1.call-update) | async-done | bytes 524304 | tf_op jit(solution)/shard_map/reduce_scatter | solution.py:301
  590.2 34.3 %psum.14 = f32[2,1024]{1,0:T(2,128)} all-reduce(f32[2,1024]{1,0:T(2,128)} %pad_maximum_fusion.12), channel_id=1, replica_groups=mesh['dp'=16,'tensor'=2] {'dp'}, use_global_device_ids=true, to_apply=%region_25.26 | all-reduce | flops 2048 | bytes 16384 | tf_op jit(solution)/shard_map/psum | solution.py:21
  624.5 6.0 psum.15
  636.2 35.8 %reduce-scatter.21.cloned.1.call-done = bf16[64,2,1312]{2,0,1:T(8,128)(2,1)} async-done(((bf16[1024,2,1312]{2,0,1:T(8,128)(2,1)}), bf16[64,2,1312]{2,0,1:T(8,128)(2,1)}) %reduce-scatter.21.cloned.1.call-update) | async-done | bytes 335888 | tf_op jit(solution)/shard_map/reduce_scatter | solution.py:319
  678.8 62.5 %reduce-scatter.17.cloned.1.call-done = bf16[64,1536]{1,0:T(8,128)(2,1)} async-done(((bf16[1024,1536]{1,0:T(8,128)(2,1)}), bf16[64,1536]{1,0:T(8,128)(2,1)}) %reduce-scatter.17.cloned.1.call-update) | async-done | bytes 196624 | tf_op jit(solution)/shard_map/reduce_scatter | solution.py:313
  (226 shorter events, 140.6 us)
Async XLA Ops:
  7.2 29.0 %all-gather.9.cloned.1.call-start = ((), (), s32[]{:S(2)}) async-start(), calls=%async_computation.8 | async-start | bytes 1572864 | tf_op jit(solution)/shard_map/all_gather | solution.py:220
  10.2 78.4 %copy-start.37 = (f32[256]{0:T(256)}, f32[256]{0:T(256)S(1)}, u32[]{:S(2)}) copy-start(f32[256]{0:T(256)S(1)} %add_rsqrt_fusion.1) | copy-start | bytes 3076
  12.1 72.5 %all-gather.11.cloned.1.call-start = ((), (), s32[]{:S(2)}) async-start(), calls=%async_computation.9 | async-start | bytes 3342336 | tf_op jit(solution)/shard_map/all_gather | solution.py:201
  12.9 112.0 %all-gather.13.cloned.1.call-start = ((), (), s32[]{:S(2)}) async-start(), calls=%async_computation.10 | async-start | bytes 1114112 | tf_op jit(solution)/shard_map/all_gather | solution.py:202
  13.6 145.7 %reduce-scatter.9.cloned.1.call-start = ((), (), s32[]{:S(2)}) async-start(), calls=%async_computation.11 | async-start | bytes 3145728 | tf_op jit(solution)/shard_map/reduce_scatter | solution.py:236
  90.3 3.9 collective-permute-start
  92.4 3.4 collective-permute-start.1
  128.2 92.5 %all-gather.17.cloned.1.call-start = ((), (), s32[]{:S(2)}) async-start(), calls=%async_computation.13 | async-start | bytes 6127616 | tf_op jit(solution)/shard_map/all_gather | solution.py:203
  129.3 113.3 %all-gather.15.cloned.1.call-start = ((), (), s32[]{:S(2)}) async-start(), calls=%async_computation.12 | async-start | bytes 1572864 | tf_op jit(solution)/shard_map/all_gather | solution.py:241
  162.0 104.1 %all-gather.21.cloned.1.call-start = ((), (), s32[]{:S(2)}) async-start(), calls=%async_computation.16 | async-start | bytes 1572864 | tf_op jit(solution)/shard_map/all_gather | solution.py:254
  162.9 173.6 %reduce-scatter.23.cloned.1.call-start = ((), (), s32[]{:S(2)}) async-start(), calls=%async_computation.23 | async-start | bytes 3063808 | tf_op jit(solution)/shard_map/reduce_scatter | solution.py:322
  271.2 113.6 %all-gather.19.cloned.1.call-start = ((), (), s32[]{:S(2)}) async-start(), calls=%async_computation.14 | async-start | bytes 3063808 | tf_op jit(solution)/shard_map/all_gather | solution.py:204
  341.6 89.0 %reduce-scatter.13.cloned.1.call-start = ((), (), s32[]{:S(2)}) async-start(), calls=%async_computation.17 | async-start | bytes 3145728 | tf_op jit(solution)/shard_map/reduce_scatter | solution.py:260
  399.9 53.9 %reduce-scatter.11.cloned.1.call-start = ((), (), s32[]{:S(2)}) async-start(), calls=%async_computation.15 | async-start | bytes 1572864 | tf_op jit(solution)/shard_map/reduce_scatter | solution.py:247
  405.3 73.4 %all-gather.23.cloned.1.call-start = ((), (), s32[]{:S(2)}) async-start(), calls=%async_computation.18 | async-start | bytes 1572864 | tf_op jit(solution)/shard_map/all_gather | solution.py:267
  457.2 107.5 %reduce-scatter.19.cloned.1.call-start = ((), (), s32[]{:S(2)}) async-start(), calls=%async_computation.21 | async-start | bytes 1114112 | tf_op jit(solution)/shard_map/reduce_scatter | solution.py:316
  499.5 10.1 %collective-permute-start.2 = (bf16[64,1024]{0,1:T(8,128)(2,1)}, bf16[64,1024]{0,1:T(8,128)(2,1)}, u32[]{:S(2)}, u32[]{:S(2)}) collective-permute-start(bf16[64,1024]{0,1:T(8,128)(2,1)} %get-tuple-element.137), channel_id=1, source_target_pairs={{0,2},{2,4},{4,6},{6,8},{8,10},{10,12},{12,14},{14,16},{16,18},{18... | collective-permute-start | bytes 393224 | tf_op jit(solution)/shard_map/ppermute | solution.py:32
  501.8 7.8 %collective-permute-start.3 = (bf16[64,1024]{0,1:T(8,128)(2,1)}, bf16[64,1024]{0,1:T(8,128)(2,1)}, u32[]{:S(2)}, u32[]{:S(2)}) collective-permute-start(bf16[64,1024]{0,1:T(8,128)(2,1)} %get-tuple-element.138), channel_id=1, source_target_pairs={{2,0},{4,2},{6,4},{8,6},{10,8},{12,10},{14,12},{16,14},{18,16},{20... | collective-permute-start | bytes 393224 | tf_op jit(solution)/shard_map/ppermute | solution.py:33
  504.9 81.9 %reduce-scatter.15.cloned.1.call-start = ((), (), s32[]{:S(2)}) async-start(), calls=%async_computation.19 | async-start | bytes 1572864 | tf_op jit(solution)/shard_map/reduce_scatter | solution.py:301
  529.7 142.3 %reduce-scatter.21.cloned.1.call-start = ((), (), s32[]{:S(2)}) async-start(), calls=%async_computation.22 | async-start | bytes 6127616 | tf_op jit(solution)/shard_map/reduce_scatter | solution.py:319
  536.2 205.0 %reduce-scatter.17.cloned.1.call-start = ((), (), s32[]{:S(2)}) async-start(), calls=%async_computation.20 | async-start | bytes 3342336 | tf_op jit(solution)/shard_map/reduce_scatter | solution.py:313
  544.8 85.6 %copy-start.36 = (f32[2,1024]{1,0:T(2,128)S(1)}, f32[2,1024]{1,0:T(2,128)}, u32[]{:S(2)}) copy-start(f32[2,1024]{1,0:T(2,128)} %param.28) | copy-start | bytes 24580
  544.8 89.0 %copy-start.9 = (f32[256,1024]{1,0:T(8,128)S(1)}, f32[256,1024]{1,0:T(8,128)}, u32[]{:S(2)}) copy-start(f32[256,1024]{1,0:T(8,128)} %get-tuple-element.127) | copy-start | bytes 3145732
  568.2 103.8 %copy-start.13 = (f32[64,2,1312]{2,1,0:T(2,128)S(1)}, f32[64,2,1312]{2,1,0:T(2,128)}, u32[]{:S(2)}) copy-start(f32[64,2,1312]{2,1,0:T(2,128)} %param.26) | copy-start | bytes 2015236
  (42 other events, 472.3 us)
Sparse Core Ops, SparseCore 0:
  12.2 23.9 all-gather.8
  39.1 45.4 all-gather.10
  87.3 37.4 all-gather.12
  128.3 30.8 reduce-scatter.8
  161.9 58.6 all-gather.16
  222.7 19.8 all-gather.14
  244.7 21.2 all-gather.20
  271.3 65.1 reduce-scatter.22
  341.7 42.9 all-gather.18
  400.0 30.5 reduce-scatter.12
  433.4 20.3 reduce-scatter.10
  457.3 21.2 all-gather.22
  505.0 59.5 reduce-scatter.18
  567.3 19.4 reduce-scatter.14
  590.6 81.3 reduce-scatter.20
  675.7 65.5 reduce-scatter.16
